TPU v7x, 32 devices: a whole 2x2x4 slice. The times are simulated.
32 devices in a mesh: px: 8 (over z, y), py: 4 (over x, core).
Axes of the slice: x: 2, y: 2, z: 4, core: 2. Of those that a mesh axis runs over, the one named last changes fastest.
Arguments:
- history: bfloat16 [8, 4, 3, 128, 384], P('px', 'py'), may hold values from -6 to 6
- incident: float32 [8, 4, 4, 128, 384], P('px', 'py'), may hold values from -6 to 6
- blocks: bfloat16 [8, 4, 32, 128, 128], P('px', 'py'), may hold values from -0.09375 to 0.09375
- self_inverse: float32 [8, 4, 128, 128], P('px', 'py'), as said below
- neighbour: int32 [8, 4, 32], P('px', 'py'), may hold values from 0 to 8
- delay: int32 [8, 4, 32], P('px', 'py'), may hold values from 1 to 3
Outputs:
- currents: bfloat16 [8, 4, 4, 128, 384], P('px', 'py')
Inputs may be any that keep to these rules, and one draw needn't show every extreme that they name: neighbour n names the source tile at row offset n // 3 - 1 and column offset n % 3 - 1. `self_inverse`: each matrix has a positive diagonal.
All inputs are finite; a program needn't handle non-finite values.
Results may differ from a plain program's by a relative error of at most 0.004.
Values may be sent and summed in bfloat16 or wider, within the bound.
A program may use at most 64 MiB of HBM per device.

v0:
```python
import jax
import jax.numpy as jnp
from jax import lax
from jax.sharding import PartitionSpec as P

STEPS = 4


def extended(cells, sides, width):
    for axis, dim in sides:
        count = lax.axis_size(axis)
        ends = count - 1
        head = lax.slice_in_dim(cells, 0, width, axis=dim)
        tail = lax.slice_in_dim(cells, cells.shape[dim] - width, cells.shape[dim], axis=dim)
        cells = jnp.concatenate(
            [
                lax.ppermute(tail, axis, [(i, (i + 1) % count) for i in range(ends)]),
                cells,
                lax.ppermute(head, axis, [((i + 1) % count, i) for i in range(ends)]),
            ],
            axis=dim,
        )
    return cells


def spread_past(past):
    return extended(past, (("px", 0), ("py", 1)), 1)


def spread_fresh(fresh):
    return extended(fresh, (("px", 0), ("py", 1)), 1)


def local(history, incident, blocks, self_inverse, neighbour, delay):
    depth = history.shape[2]
    basis = history.shape[3]
    ports = history.shape[4]
    past = jnp.flip(history, axis=2)
    frames = [spread_past(past)]
    ids = neighbour[0, 0]
    lags = delay[0, 0]
    matrix = blocks[0, 0]
    inverse = self_inverse[0, 0]
    results = []
    for step in range(STEPS):
        stack = jnp.concatenate(frames, axis=2)
        count = stack.shape[2]
        flat = stack.reshape(9 * count, basis, ports)
        index = ids * count + (step - lags + depth)
        sources = jnp.take(flat, index, axis=0)
        field = jnp.einsum("jab,jbp->ap", matrix, sources, preferred_element_type=jnp.float32)
        rhs = incident[0, 0, step] - field
        current = jnp.dot(
            inverse, rhs, precision=lax.Precision.HIGHEST, preferred_element_type=jnp.float32
        ).astype(jnp.bfloat16)
        results.append(current)
        if step + 1 < STEPS:
            frames.append(spread_fresh(current[None, None])[:, :, None])
    return jnp.stack(results, axis=0)[None, None]


def solution(mesh):
    in_specs = (
        P("px", "py", None, None, None),
        P("px", "py", None, None, None),
        P("px", "py", None, None, None),
        P("px", "py", None, None),
        P("px", "py", None),
        P("px", "py", None),
    )
    out_specs = P("px", "py", None, None, None)
    return jax.shard_map(local, mesh=mesh, in_specs=in_specs, out_specs=out_specs, check_vma=False)
```

profile of v0, /device:TPU:9, one launch (start us, length us, event | category | flops | bytes accessed | tf_op | source)
XLA Modules:
  0.0 152.8 jit_solution(5252236934776318238)
XLA Ops:
  1.1 3.0 %collective-permute-start.1 = (bf16[1,1,3,128,384]{4,3,2,1,0:T(8,128)(2,1)S(1)}, bf16[1,1,3,128,384]{4,3,2,1,0:T(8,128)(2,1)S(1)}, u32[]{:S(2)}, u32[]{:S(2)}) collective-permute-start(bf16[1,1,3,128,384]{4,3,2,1,0:T(8,128)(2,1)S(1)} %rev.4), channel_id=1, source_target_pairs={{4,0},{8,4},{12,8},{16,12},{20,16},{24,20},{28,24},{5,1},{9,5},{13... | collective-permute-start | bytes 884744 | tf_op jit(solution)/shard_map/ppermute | solution.py:19
  4.1 2.2 %collective-permute-start = (bf16[1,1,3,128,384]{4,3,2,1,0:T(8,128)(2,1)S(1)}, bf16[1,1,3,128,384]{4,3,2,1,0:T(8,128)(2,1)S(1)}, u32[]{:S(2)}, u32[]{:S(2)}) collective-permute-start(bf16[1,1,3,128,384]{4,3,2,1,0:T(8,128)(2,1)S(1)} %rev.4), channel_id=1, source_target_pairs={{0,4},{4,8},{8,12},{12,16},{16,20},{20,24},{24,28},{1,5},{5,9},{9,... | collective-permute-start | bytes 884744 | tf_op jit(solution)/shard_map/ppermute | solution.py:17
  6.4 10.8 %collective-permute-done.1 = bf16[1,1,3,128,384]{4,3,2,1,0:T(8,128)(2,1)S(1)} collective-permute-done((bf16[1,1,3,128,384]{4,3,2,1,0:T(8,128)(2,1)S(1)}, bf16[1,1,3,128,384]{4,3,2,1,0:T(8,128)(2,1)S(1)}, u32[]{:S(2)}, u32[]{:S(2)}) %collective-permute-start.1) | collective-permute-done | bytes 294944 | tf_op jit(solution)/shard_map/ppermute | solution.py:19
  18.3 2.5 %collective-permute-start.3 = (bf16[3,1,3,128,384]{4,3,2,1,0:T(8,128)(2,1)S(1)}, bf16[3,1,3,128,384]{4,3,2,1,0:T(8,128)(2,1)S(1)}, u32[]{:S(2)}, u32[]{:S(2)}) collective-permute-start(bf16[3,1,3,128,384]{4,3,2,1,0:T(8,128)(2,1)S(1)} %pad_maximum_fusion.4), channel_id=1, source_target_pairs={{1,0},{2,1},{3,2},{5,4},{6,5},{7,6},{9,8},{10,9},{11,10},{13,12},{... | collective-permute-start | bytes 2654216 | tf_op jit(solution)/shard_map/ppermute | solution.py:19
  20.8 3.1 %collective-permute-start.2 = (bf16[3,1,3,128,384]{4,3,2,1,0:T(8,128)(2,1)S(1)}, bf16[3,1,3,128,384]{4,3,2,1,0:T(8,128)(2,1)S(1)}, u32[]{:S(2)}, u32[]{:S(2)}) collective-permute-start(bf16[3,1,3,128,384]{4,3,2,1,0:T(8,128)(2,1)S(1)} %pad_maximum_fusion.4), channel_id=1, source_target_pairs={{0,1},{1,2},{2,3},{4,5},{5,6},{6,7},{8,9},{9,10},{10,11},{12,13},{... | collective-permute-start | bytes 2654216 | tf_op jit(solution)/shard_map/ppermute | solution.py:17
  25.3 7.4 %collective-permute-done.3 = bf16[3,1,3,128,384]{4,3,2,1,0:T(8,128)(2,1)S(1)} collective-permute-done((bf16[3,1,3,128,384]{4,3,2,1,0:T(8,128)(2,1)S(1)}, bf16[3,1,3,128,384]{4,3,2,1,0:T(8,128)(2,1)S(1)}, u32[]{:S(2)}, u32[]{:S(2)}) %collective-permute-start.3) | collective-permute-done | bytes 884768 | tf_op jit(solution)/shard_map/ppermute | solution.py:19
  36.6 4.4 %gather_fusion = bf16[32,128,384]{2,1,0:T(8,128)(2,1)} fusion(bf16[27,128,384]{2,1,0:T(8,128)(2,1)} %bitcast.111, s32[1024]{0:T(1024)S(1)} %get-tuple-element.16), kind=kCustom, calls=%fused_computation | custom fusion | bytes 6291584 | tf_op jit(solution)/shard_map/jit(_take)/gather | solution.py:50
  40.9 2.7 %fusion.37 = f32[128,384]{1,0:T(8,128)S(1)} fusion(bf16[32,128,384]{2,1,0:T(8,128)(2,1)} %gather_fusion, pred[32]{0:T(512)(128)(4,1)S(1)} %get-tuple-element.7, bf16[1,1,32,128,128]{4,3,2,1,0:T(8,128)(2,1)S(1)} %copy-done, f32[1,1,4,128,384]{4,3,2,1,0:T(8,128)} %param.7), kind=kOutput, calls=%fused_computation.31 | convolution fusion | flops 404275200 | bytes 4587552 | tf_op jit(solution)/shard_map/jab,jbp->ap/dot_general | solution.py:51
  44.2 4.0 %collective-permute-start.5 = (bf16[1,1,128,384]{2,3,1,0:T(8,128)(2,1)S(1)}, bf16[1,1,128,384]{2,3,1,0:T(8,128)(2,1)S(1)}, u32[]{:S(2)}, u32[]{:S(2)}) collective-permute-start(bf16[1,1,128,384]{2,3,1,0:T(8,128)(2,1)S(1)} %bitcast.113), channel_id=1, source_target_pairs={{4,0},{8,4},{12,8},{16,12},{20,16},{24,20},{28,24},{5,1},{9,5},{13... | collective-permute-start | bytes 294920 | tf_op jit(solution)/shard_map/ppermute | solution.py:19
  50.3 4.2 %collective-permute-done.4 = bf16[1,1,128,384]{2,3,1,0:T(8,128)(2,1)S(1)} collective-permute-done((bf16[1,1,128,384]{2,3,1,0:T(8,128)(2,1)S(1)}, bf16[1,1,128,384]{2,3,1,0:T(8,128)(2,1)S(1)}, u32[]{:S(2)}, u32[]{:S(2)}) %collective-permute-start.4) | collective-permute-done | bytes 98336 | tf_op jit(solution)/shard_map/ppermute | solution.py:17
  56.4 5.8 %collective-permute-start.6 = (bf16[3,1,128,384]{2,3,1,0:T(8,128)(2,1)S(1)}, bf16[3,1,128,384]{2,3,1,0:T(8,128)(2,1)S(1)}, u32[]{:S(2)}, u32[]{:S(2)}) collective-permute-start(bf16[3,1,128,384]{2,3,1,0:T(8,128)(2,1)S(1)} %pad_maximum_fusion.5), channel_id=1, source_target_pairs={{0,1},{1,2},{2,3},{4,5},{5,6},{6,7},{8,9},{9,10},{10,11},{12,13},{... | collective-permute-start | bytes 884744 | tf_op jit(solution)/shard_map/ppermute | solution.py:17
  62.2 2.5 %collective-permute-done.7 = bf16[3,1,128,384]{2,3,1,0:T(8,128)(2,1)S(1)} collective-permute-done((bf16[3,1,128,384]{2,3,1,0:T(8,128)(2,1)S(1)}, bf16[3,1,128,384]{2,3,1,0:T(8,128)(2,1)S(1)}, u32[]{:S(2)}, u32[]{:S(2)}) %collective-permute-start.7) | collective-permute-done | bytes 294944 | tf_op jit(solution)/shard_map/ppermute | solution.py:19
  66.9 2.5 %copy.7 = bf16[3,3,1,128,384]{4,3,2,1,0:T(8,128)(2,1)S(1)} copy(bf16[3,3,1,128,384]{3,4,1,0,2:T(8,128)(2,1)} %maximum_bitcast_fusion) | data formatting | bytes 1769472 | tf_op jit(solution)/shard_map/broadcast_in_dim | solution.py:58
  69.4 3.2 %pad_maximum_fusion.2 = bf16[3,3,4,128,384]{4,3,2,1,0:T(8,128)(2,1)} fusion(bf16[3,3,1,128,384]{4,3,2,1,0:T(8,128)(2,1)S(1)} %copy.7, bf16[3,1,3,128,384]{4,3,2,1,0:T(8,128)(2,1)S(1)} %collective-permute-done.3, bf16[1,1,3,128,384]{4,3,2,1,0:T(8,128)(2,1)S(1)} %collective-permute-done.1, bf16[1,1,3,128,384]{4,3,2,1,0:T(8,128)(2,1)S(1)} %rev.4, ...), kind=kLoop, calls=%fused_computation.6 | loop fusion | flops 8847360 | bytes 7077888 | tf_op jit(solution)/shard_map/concatenate | solution.py:46
  72.5 4.6 %gather_fusion.1 = bf16[32,128,384]{2,1,0:T(8,128)(2,1)} fusion(bf16[36,128,384]{2,1,0:T(8,128)(2,1)} %bitcast.112, s32[1024]{0:T(1024)S(1)} %get-tuple-element.15), kind=kCustom, calls=%fused_computation.1 | custom fusion | bytes 6291584 | tf_op jit(solution)/shard_map/jit(_take)/gather | solution.py:50
  77.2 2.7 %fusion.34 = f32[128,384]{1,0:T(8,128)S(1)} fusion(bf16[32,128,384]{2,1,0:T(8,128)(2,1)} %gather_fusion.1, pred[32]{0:T(512)(128)(4,1)S(1)} %get-tuple-element.6, bf16[1,1,32,128,128]{4,3,2,1,0:T(8,128)(2,1)S(1)} %copy-done, f32[1,1,4,128,384]{4,3,2,1,0:T(8,128)} %param.7), kind=kOutput, calls=%fused_computation.30 | convolution fusion | flops 404275200 | bytes 4587552 | tf_op jit(solution)/shard_map/jab,jbp->ap/dot_general | solution.py:51
  82.4 3.4 %collective-permute-start.8 = (bf16[1,1,128,384]{2,3,1,0:T(8,128)(2,1)S(1)}, bf16[1,1,128,384]{2,3,1,0:T(8,128)(2,1)S(1)}, u32[]{:S(2)}, u32[]{:S(2)}) collective-permute-start(bf16[1,1,128,384]{2,3,1,0:T(8,128)(2,1)S(1)} %bitcast.119), channel_id=1, source_target_pairs={{0,4},{4,8},{8,12},{12,16},{16,20},{20,24},{24,28},{1,5},{5,9},{9,... | collective-permute-start | bytes 294920 | tf_op jit(solution)/shard_map/ppermute | solution.py:17
  85.8 2.8 %collective-permute-done.8 = bf16[1,1,128,384]{2,3,1,0:T(8,128)(2,1)S(1)} collective-permute-done((bf16[1,1,128,384]{2,3,1,0:T(8,128)(2,1)S(1)}, bf16[1,1,128,384]{2,3,1,0:T(8,128)(2,1)S(1)}, u32[]{:S(2)}, u32[]{:S(2)}) %collective-permute-start.8) | collective-permute-done | bytes 98336 | tf_op jit(solution)/shard_map/ppermute | solution.py:17
  90.6 5.5 %collective-permute-start.10 = (bf16[3,1,128,384]{2,3,1,0:T(8,128)(2,1)S(1)}, bf16[3,1,128,384]{2,3,1,0:T(8,128)(2,1)S(1)}, u32[]{:S(2)}, u32[]{:S(2)}) collective-permute-start(bf16[3,1,128,384]{2,3,1,0:T(8,128)(2,1)S(1)} %pad_maximum_fusion.6), channel_id=1, source_target_pairs={{0,1},{1,2},{2,3},{4,5},{5,6},{6,7},{8,9},{9,10},{10,11},{12,13},{... | collective-permute-start | bytes 884744 | tf_op jit(solution)/shard_map/ppermute | solution.py:17
  96.2 2.4 %collective-permute-done.11 = bf16[3,1,128,384]{2,3,1,0:T(8,128)(2,1)S(1)} collective-permute-done((bf16[3,1,128,384]{2,3,1,0:T(8,128)(2,1)S(1)}, bf16[3,1,128,384]{2,3,1,0:T(8,128)(2,1)S(1)}, u32[]{:S(2)}, u32[]{:S(2)}) %collective-permute-start.11) | collective-permute-done | bytes 294944 | tf_op jit(solution)/shard_map/ppermute | solution.py:19
  100.8 2.3 %copy.9 = bf16[3,3,1,128,384]{4,3,2,1,0:T(8,128)(2,1)} copy(bf16[3,3,1,128,384]{3,4,1,0,2:T(8,128)(2,1)} %maximum_bitcast_fusion.1) | data formatting | bytes 1769472 | tf_op jit(solution)/shard_map/broadcast_in_dim | solution.py:58
  103.1 4.4 %pad_maximum_fusion.1 = bf16[3,3,5,128,384]{4,3,2,1,0:T(8,128)(2,1)} fusion(bf16[3,3,1,128,384]{4,3,2,1,0:T(8,128)(2,1)} %copy.9, bf16[3,3,1,128,384]{4,3,2,1,0:T(8,128)(2,1)S(1)} %copy.7, bf16[3,1,3,128,384]{4,3,2,1,0:T(8,128)(2,1)S(1)} %collective-permute-done.3, bf16[1,1,3,128,384]{4,3,2,1,0:T(8,128)(2,1)S(1)} %collective-permute-done.1, ...), kind=kLoop, calls=%fused_computation.5 | loop fusion | flops 13271040 | bytes 8847360 | tf_op jit(solution)/shard_map/concatenate | solution.py:46
  107.5 4.9 %gather_fusion.2 = bf16[32,128,384]{2,1,0:T(8,128)(2,1)} fusion(bf16[45,128,384]{2,1,0:T(8,128)(2,1)} %bitcast.110, s32[1024]{0:T(1024)S(1)} %get-tuple-element.14), kind=kCustom, calls=%fused_computation.2 | custom fusion | bytes 6291584 | tf_op jit(solution)/shard_map/jit(_take)/gather | solution.py:50
  112.4 2.7 %fusion.31 = f32[128,384]{1,0:T(8,128)S(1)} fusion(bf16[32,128,384]{2,1,0:T(8,128)(2,1)} %gather_fusion.2, pred[32]{0:T(512)(128)(4,1)S(1)} %get-tuple-element.8, bf16[1,1,32,128,128]{4,3,2,1,0:T(8,128)(2,1)S(1)} %copy-done, f32[1,1,4,128,384]{4,3,2,1,0:T(8,128)} %param.7), kind=kOutput, calls=%fused_computation.29 | convolution fusion | flops 404275200 | bytes 4587552 | tf_op jit(solution)/shard_map/jab,jbp->ap/dot_general | solution.py:51
  117.6 3.4 %collective-permute-start.12 = (bf16[1,1,128,384]{2,3,1,0:T(8,128)(2,1)S(1)}, bf16[1,1,128,384]{2,3,1,0:T(8,128)(2,1)S(1)}, u32[]{:S(2)}, u32[]{:S(2)}) collective-permute-start(bf16[1,1,128,384]{2,3,1,0:T(8,128)(2,1)S(1)} %bitcast.124), channel_id=1, source_target_pairs={{0,4},{4,8},{8,12},{12,16},{16,20},{20,24},{24,28},{1,5},{5,9},{9,... | collective-permute-start | bytes 294920 | tf_op jit(solution)/shard_map/ppermute | solution.py:17
  121.0 2.8 %collective-permute-done.12 = bf16[1,1,128,384]{2,3,1,0:T(8,128)(2,1)S(1)} collective-permute-done((bf16[1,1,128,384]{2,3,1,0:T(8,128)(2,1)S(1)}, bf16[1,1,128,384]{2,3,1,0:T(8,128)(2,1)S(1)}, u32[]{:S(2)}, u32[]{:S(2)}) %collective-permute-start.12) | collective-permute-done | bytes 98336 | tf_op jit(solution)/shard_map/ppermute | solution.py:17
  125.8 5.5 %collective-permute-start.14 = (bf16[3,1,128,384]{2,3,1,0:T(8,128)(2,1)S(1)}, bf16[3,1,128,384]{2,3,1,0:T(8,128)(2,1)S(1)}, u32[]{:S(2)}, u32[]{:S(2)}) collective-permute-start(bf16[3,1,128,384]{2,3,1,0:T(8,128)(2,1)S(1)} %pad_maximum_fusion.7), channel_id=1, source_target_pairs={{0,1},{1,2},{2,3},{4,5},{5,6},{6,7},{8,9},{9,10},{10,11},{12,13},{... | collective-permute-start | bytes 884744 | tf_op jit(solution)/shard_map/ppermute | solution.py:17
  131.3 2.5 %collective-permute-done.15 = bf16[3,1,128,384]{2,3,1,0:T(8,128)(2,1)S(1)} collective-permute-done((bf16[3,1,128,384]{2,3,1,0:T(8,128)(2,1)S(1)}, bf16[3,1,128,384]{2,3,1,0:T(8,128)(2,1)S(1)}, u32[]{:S(2)}, u32[]{:S(2)}) %collective-permute-start.15) | collective-permute-done | bytes 294944 | tf_op jit(solution)/shard_map/ppermute | solution.py:19
  136.0 2.3 %copy.12 = bf16[3,3,1,128,384]{4,3,2,1,0:T(8,128)(2,1)} copy(bf16[3,3,1,128,384]{3,4,1,0,2:T(8,128)(2,1)} %maximum_bitcast_fusion.2) | data formatting | bytes 1769472 | tf_op jit(solution)/shard_map/broadcast_in_dim | solution.py:58
  138.3 5.0 %pad_maximum_fusion = bf16[3,3,6,128,384]{4,3,2,1,0:T(8,128)(2,1)} fusion(bf16[3,3,1,128,384]{4,3,2,1,0:T(8,128)(2,1)} %copy.12, bf16[3,3,1,128,384]{4,3,2,1,0:T(8,128)(2,1)} %copy.9, bf16[3,3,1,128,384]{4,3,2,1,0:T(8,128)(2,1)S(1)} %copy.7, bf16[3,1,3,128,384]{4,3,2,1,0:T(8,128)(2,1)S(1)} %collective-permute-done.3, ...), kind=kLoop, calls=%fused_computation.4 | loop fusion | flops 18579456 | bytes 10616832 | tf_op jit(solution)/shard_map/concatenate | solution.py:46
  143.3 5.2 %gather_fusion.3 = bf16[32,128,384]{2,1,0:T(8,128)(2,1)} fusion(bf16[54,128,384]{2,1,0:T(8,128)(2,1)} %bitcast.109, s32[1024]{0:T(1024)S(1)} %get-tuple-element.13), kind=kCustom, calls=%fused_computation.3 | custom fusion | bytes 6291584 | tf_op jit(solution)/shard_map/jit(_take)/gather | solution.py:50
  148.5 2.7 %fusion.28 = f32[128,384]{1,0:T(8,128)S(1)} fusion(bf16[32,128,384]{2,1,0:T(8,128)(2,1)} %gather_fusion.3, pred[32]{0:T(512)(128)(4,1)S(1)} %get-tuple-element.5, bf16[1,1,32,128,128]{4,3,2,1,0:T(8,128)(2,1)S(1)} %copy-done, f32[1,1,4,128,384]{4,3,2,1,0:T(8,128)} %param.7), kind=kOutput, calls=%fused_computation.28 | convolution fusion | flops 404275200 | bytes 4587552 | tf_op jit(solution)/shard_map/jab,jbp->ap/dot_general | solution.py:51
  (55 shorter events, 29.0 us)
Async XLA Ops:
  0.0 40.9 %copy-start = (bf16[1,1,32,128,128]{4,3,2,1,0:T(8,128)(2,1)S(1)}, bf16[1,1,32,128,128]{4,3,2,1,0:T(8,128)(2,1)}, u32[]{:S(2)}) copy-start(bf16[1,1,32,128,128]{4,3,2,1,0:T(8,128)(2,1)} %param.8) | copy-start | bytes 3145732
  1.1 16.1 %collective-permute-start.1 = (bf16[1,1,3,128,384]{4,3,2,1,0:T(8,128)(2,1)S(1)}, bf16[1,1,3,128,384]{4,3,2,1,0:T(8,128)(2,1)S(1)}, u32[]{:S(2)}, u32[]{:S(2)}) collective-permute-start(bf16[1,1,3,128,384]{4,3,2,1,0:T(8,128)(2,1)S(1)} %rev.4), channel_id=1, source_target_pairs={{4,0},{8,4},{12,8},{16,12},{20,16},{24,20},{28,24},{5,1},{9,5},{13... | collective-permute-start | bytes 884744 | tf_op jit(solution)/shard_map/ppermute | solution.py:19
  4.1 14.0 %collective-permute-start = (bf16[1,1,3,128,384]{4,3,2,1,0:T(8,128)(2,1)S(1)}, bf16[1,1,3,128,384]{4,3,2,1,0:T(8,128)(2,1)S(1)}, u32[]{:S(2)}, u32[]{:S(2)}) collective-permute-start(bf16[1,1,3,128,384]{4,3,2,1,0:T(8,128)(2,1)S(1)} %rev.4), channel_id=1, source_target_pairs={{0,4},{4,8},{8,12},{12,16},{16,20},{20,24},{24,28},{1,5},{5,9},{9,... | collective-permute-start | bytes 884744 | tf_op jit(solution)/shard_map/ppermute | solution.py:17
  18.2 18.4 %copy-start.2 = (bf16[1,1,3,128,384]{4,3,2,1,0:T(8,128)(2,1)}, bf16[1,1,3,128,384]{4,3,2,1,0:T(8,128)(2,1)S(1)}, u32[]{:S(2)}) copy-start(bf16[1,1,3,128,384]{4,3,2,1,0:T(8,128)(2,1)S(1)} %collective-permute-done) | copy-start | bytes 884740
  18.3 14.4 %collective-permute-start.3 = (bf16[3,1,3,128,384]{4,3,2,1,0:T(8,128)(2,1)S(1)}, bf16[3,1,3,128,384]{4,3,2,1,0:T(8,128)(2,1)S(1)}, u32[]{:S(2)}, u32[]{:S(2)}) collective-permute-start(bf16[3,1,3,128,384]{4,3,2,1,0:T(8,128)(2,1)S(1)} %pad_maximum_fusion.4), channel_id=1, source_target_pairs={{1,0},{2,1},{3,2},{5,4},{6,5},{7,6},{9,8},{10,9},{11,10},{13,12},{... | collective-permute-start | bytes 2654216 | tf_op jit(solution)/shard_map/ppermute | solution.py:19
  20.8 13.1 %collective-permute-start.2 = (bf16[3,1,3,128,384]{4,3,2,1,0:T(8,128)(2,1)S(1)}, bf16[3,1,3,128,384]{4,3,2,1,0:T(8,128)(2,1)S(1)}, u32[]{:S(2)}, u32[]{:S(2)}) collective-permute-start(bf16[3,1,3,128,384]{4,3,2,1,0:T(8,128)(2,1)S(1)} %pad_maximum_fusion.4), channel_id=1, source_target_pairs={{0,1},{1,2},{2,3},{4,5},{5,6},{6,7},{8,9},{9,10},{10,11},{12,13},{... | collective-permute-start | bytes 2654216 | tf_op jit(solution)/shard_map/ppermute | solution.py:17
  33.8 1.0 copy-start.1
  40.9 2.7 %copy-start.7 = (f32[1,1,128,128]{3,2,1,0:T(8,128)S(1)}, f32[1,1,128,128]{3,2,1,0:T(8,128)}, u32[]{:S(2)}) copy-start(f32[1,1,128,128]{3,2,1,0:T(8,128)} %param.9) | copy-start | bytes 196612
  44.2 6.1 %collective-permute-start.5 = (bf16[1,1,128,384]{2,3,1,0:T(8,128)(2,1)S(1)}, bf16[1,1,128,384]{2,3,1,0:T(8,128)(2,1)S(1)}, u32[]{:S(2)}, u32[]{:S(2)}) collective-permute-start(bf16[1,1,128,384]{2,3,1,0:T(8,128)(2,1)S(1)} %bitcast.113), channel_id=1, source_target_pairs={{4,0},{8,4},{12,8},{16,12},{20,16},{24,20},{28,24},{5,1},{9,5},{13... | collective-permute-start | bytes 294920 | tf_op jit(solution)/shard_map/ppermute | solution.py:19
  48.2 6.3 %collective-permute-start.4 = (bf16[1,1,128,384]{2,3,1,0:T(8,128)(2,1)S(1)}, bf16[1,1,128,384]{2,3,1,0:T(8,128)(2,1)S(1)}, u32[]{:S(2)}, u32[]{:S(2)}) collective-permute-start(bf16[1,1,128,384]{2,3,1,0:T(8,128)(2,1)S(1)} %bitcast.114), channel_id=1, source_target_pairs={{0,4},{4,8},{8,12},{12,16},{16,20},{20,24},{24,28},{1,5},{5,9},{9,... | collective-permute-start | bytes 294920 | tf_op jit(solution)/shard_map/ppermute | solution.py:17
  54.5 10.2 %collective-permute-start.7 = (bf16[3,1,128,384]{2,3,1,0:T(8,128)(2,1)S(1)}, bf16[3,1,128,384]{2,3,1,0:T(8,128)(2,1)S(1)}, u32[]{:S(2)}, u32[]{:S(2)}) collective-permute-start(bf16[3,1,128,384]{2,3,1,0:T(8,128)(2,1)S(1)} %pad_maximum_fusion.5), channel_id=1, source_target_pairs={{1,0},{2,1},{3,2},{5,4},{6,5},{7,6},{9,8},{10,9},{11,10},{13,12},{... | collective-permute-start | bytes 884744 | tf_op jit(solution)/shard_map/ppermute | solution.py:19
  56.4 9.5 %collective-permute-start.6 = (bf16[3,1,128,384]{2,3,1,0:T(8,128)(2,1)S(1)}, bf16[3,1,128,384]{2,3,1,0:T(8,128)(2,1)S(1)}, u32[]{:S(2)}, u32[]{:S(2)}) collective-permute-start(bf16[3,1,128,384]{2,3,1,0:T(8,128)(2,1)S(1)} %pad_maximum_fusion.5), channel_id=1, source_target_pairs={{0,1},{1,2},{2,3},{4,5},{5,6},{6,7},{8,9},{9,10},{10,11},{12,13},{... | collective-permute-start | bytes 884744 | tf_op jit(solution)/shard_map/ppermute | solution.py:17
  77.2 2.7 %copy-start.8 = (f32[1,1,128,128]{3,2,1,0:T(8,128)S(1)}, f32[1,1,128,128]{3,2,1,0:T(8,128)}, u32[]{:S(2)}) copy-start(f32[1,1,128,128]{3,2,1,0:T(8,128)} %param.9) | copy-start | bytes 196612
  80.4 19.4 %copy-start.3 = (bf16[384,128]{1,0:T(8,128)(2,1)}, bf16[384,128]{1,0:T(8,128)(2,1)S(1)}, u32[]{:S(2)}) copy-start(bf16[384,128]{1,0:T(8,128)(2,1)S(1)} %convolution_convert_fusion.2) | copy-start | bytes 294916
  80.4 5.4 %collective-permute-start.9 = (bf16[1,1,128,384]{2,3,1,0:T(8,128)(2,1)S(1)}, bf16[1,1,128,384]{2,3,1,0:T(8,128)(2,1)S(1)}, u32[]{:S(2)}, u32[]{:S(2)}) collective-permute-start(bf16[1,1,128,384]{2,3,1,0:T(8,128)(2,1)S(1)} %bitcast.118), channel_id=1, source_target_pairs={{4,0},{8,4},{12,8},{16,12},{20,16},{24,20},{28,24},{5,1},{9,5},{13... | collective-permute-start | bytes 294920 | tf_op jit(solution)/shard_map/ppermute | solution.py:19
  82.4 6.3 %collective-permute-start.8 = (bf16[1,1,128,384]{2,3,1,0:T(8,128)(2,1)S(1)}, bf16[1,1,128,384]{2,3,1,0:T(8,128)(2,1)S(1)}, u32[]{:S(2)}, u32[]{:S(2)}) collective-permute-start(bf16[1,1,128,384]{2,3,1,0:T(8,128)(2,1)S(1)} %bitcast.119), channel_id=1, source_target_pairs={{0,4},{4,8},{8,12},{12,16},{16,20},{20,24},{24,28},{1,5},{5,9},{9,... | collective-permute-start | bytes 294920 | tf_op jit(solution)/shard_map/ppermute | solution.py:17
  88.7 9.9 %collective-permute-start.11 = (bf16[3,1,128,384]{2,3,1,0:T(8,128)(2,1)S(1)}, bf16[3,1,128,384]{2,3,1,0:T(8,128)(2,1)S(1)}, u32[]{:S(2)}, u32[]{:S(2)}) collective-permute-start(bf16[3,1,128,384]{2,3,1,0:T(8,128)(2,1)S(1)} %pad_maximum_fusion.6), channel_id=1, source_target_pairs={{1,0},{2,1},{3,2},{5,4},{6,5},{7,6},{9,8},{10,9},{11,10},{13,12},{... | collective-permute-start | bytes 884744 | tf_op jit(solution)/shard_map/ppermute | solution.py:19
  90.6 9.2 %collective-permute-start.10 = (bf16[3,1,128,384]{2,3,1,0:T(8,128)(2,1)S(1)}, bf16[3,1,128,384]{2,3,1,0:T(8,128)(2,1)S(1)}, u32[]{:S(2)}, u32[]{:S(2)}) collective-permute-start(bf16[3,1,128,384]{2,3,1,0:T(8,128)(2,1)S(1)} %pad_maximum_fusion.6), channel_id=1, source_target_pairs={{0,1},{1,2},{2,3},{4,5},{5,6},{6,7},{8,9},{9,10},{10,11},{12,13},{... | collective-permute-start | bytes 884744 | tf_op jit(solution)/shard_map/ppermute | solution.py:17
  112.4 2.7 %copy-start.9 = (f32[1,1,128,128]{3,2,1,0:T(8,128)S(1)}, f32[1,1,128,128]{3,2,1,0:T(8,128)}, u32[]{:S(2)}) copy-start(f32[1,1,128,128]{3,2,1,0:T(8,128)} %param.9) | copy-start | bytes 196612
  115.6 19.4 %copy-start.5 = (bf16[384,128]{1,0:T(8,128)(2,1)}, bf16[384,128]{1,0:T(8,128)(2,1)S(1)}, u32[]{:S(2)}) copy-start(bf16[384,128]{1,0:T(8,128)(2,1)S(1)} %convolution_convert_fusion.1) | copy-start | bytes 294916
  115.6 5.4 %collective-permute-start.13 = (bf16[1,1,128,384]{2,3,1,0:T(8,128)(2,1)S(1)}, bf16[1,1,128,384]{2,3,1,0:T(8,128)(2,1)S(1)}, u32[]{:S(2)}, u32[]{:S(2)}) collective-permute-start(bf16[1,1,128,384]{2,3,1,0:T(8,128)(2,1)S(1)} %bitcast.123), channel_id=1, source_target_pairs={{4,0},{8,4},{12,8},{16,12},{20,16},{24,20},{28,24},{5,1},{9,5},{13... | collective-permute-start | bytes 294920 | tf_op jit(solution)/shard_map/ppermute | solution.py:19
  117.6 6.3 %collective-permute-start.12 = (bf16[1,1,128,384]{2,3,1,0:T(8,128)(2,1)S(1)}, bf16[1,1,128,384]{2,3,1,0:T(8,128)(2,1)S(1)}, u32[]{:S(2)}, u32[]{:S(2)}) collective-permute-start(bf16[1,1,128,384]{2,3,1,0:T(8,128)(2,1)S(1)} %bitcast.124), channel_id=1, source_target_pairs={{0,4},{4,8},{8,12},{12,16},{16,20},{20,24},{24,28},{1,5},{5,9},{9,... | collective-permute-start | bytes 294920 | tf_op jit(solution)/shard_map/ppermute | solution.py:17
  123.9 9.9 %collective-permute-start.15 = (bf16[3,1,128,384]{2,3,1,0:T(8,128)(2,1)S(1)}, bf16[3,1,128,384]{2,3,1,0:T(8,128)(2,1)S(1)}, u32[]{:S(2)}, u32[]{:S(2)}) collective-permute-start(bf16[3,1,128,384]{2,3,1,0:T(8,128)(2,1)S(1)} %pad_maximum_fusion.7), channel_id=1, source_target_pairs={{1,0},{2,1},{3,2},{5,4},{6,5},{7,6},{9,8},{10,9},{11,10},{13,12},{... | collective-permute-start | bytes 884744 | tf_op jit(solution)/shard_map/ppermute | solution.py:19
  125.8 9.2 %collective-permute-start.14 = (bf16[3,1,128,384]{2,3,1,0:T(8,128)(2,1)S(1)}, bf16[3,1,128,384]{2,3,1,0:T(8,128)(2,1)S(1)}, u32[]{:S(2)}, u32[]{:S(2)}) collective-permute-start(bf16[3,1,128,384]{2,3,1,0:T(8,128)(2,1)S(1)} %pad_maximum_fusion.7), channel_id=1, source_target_pairs={{0,1},{1,2},{2,3},{4,5},{5,6},{6,7},{8,9},{9,10},{10,11},{12,13},{... | collective-permute-start | bytes 884744 | tf_op jit(solution)/shard_map/ppermute | solution.py:17
  148.5 2.8 %copy-start.10 = (f32[1,1,128,128]{3,2,1,0:T(8,128)S(1)}, f32[1,1,128,128]{3,2,1,0:T(8,128)}, u32[]{:S(2)}) copy-start(f32[1,1,128,128]{3,2,1,0:T(8,128)} %param.9) | copy-start | bytes 196612
  148.5 3.3 %copy-start.4 = (bf16[384,128]{1,0:T(8,128)(2,1)S(1)}, bf16[384,128]{1,0:T(8,128)(2,1)}, u32[]{:S(2)}) copy-start(bf16[384,128]{1,0:T(8,128)(2,1)} %copy-done.3) | copy-start | bytes 294916
  148.5 3.3 %copy-start.6 = (bf16[384,128]{1,0:T(8,128)(2,1)S(1)}, bf16[384,128]{1,0:T(8,128)(2,1)}, u32[]{:S(2)}) copy-start(bf16[384,128]{1,0:T(8,128)(2,1)} %copy-done.5) | copy-start | bytes 294916
where the time goes:
time: 155 us; the launch traced here: 153 us
  starting transfers between devices  50.1 us (32%)
  waiting for transfers between devices  41.3 us (27%)
  local copies, waits for them, and re-layouts  29.1 us (19%)
  other arithmetic  19.1 us (12%)
  matrix products  12.9 us (8%)
    ppermute x8, starting transfers between devices, extended(): lax.ppermute(tail, axis, [(i, (i + 1) % count) for i in range(ends)])  31 us
    ppermute x8, waiting for transfers between devices, extended(): lax.ppermute(head, axis, [((i + 1) % count, i) for i in range(ends)])  25.8 us
    ppermute x8, starting transfers between devices, extended(): lax.ppermute(head, axis, [((i + 1) % count, i) for i in range(ends)])  19.1 us
    gather x4, local copies, waits for them, and re-layouts, local(): sources = jnp.take(flat, index, axis=0)  19.1 us
    ppermute x8, waiting for transfers between devices, extended(): lax.ppermute(tail, axis, [(i, (i + 1) % count) for i in range(ends)])  15.5 us
    concatenate x3, other arithmetic, local(): stack = jnp.concatenate(frames, axis=2)  12.6 us
    dot_general x4, matrix products, local(): jnp.einsum('jab,jbp->ap', matrix, sources, preferred_element_type=jnp.flo...  10.9 us
    broadcast_in_dim x3, local copies, waits for them, and re-layouts, local(): frames.append(spread_fresh(current[None, None])[:, :, None])  7.01 us
  transfers between devices with their start and end apart: 16, of which 16 were waited for; matrix products, arithmetic and copies ran while one was open for 1% of the time, Pallas kernels for 0%

commit v1 on v0

v1 whole, which is shorter than its diff:
```python
import functools

import jax
import jax.numpy as jnp
from jax import lax
from jax.experimental import pallas as pl
from jax.experimental.pallas import tpu as pltpu
from jax.sharding import PartitionSpec as P

MESH = pl.DeviceIdType.MESH
LANES = 128
GROUP = 4


def kernel(
    rows,
    cols,
    near_ref,
    lag_ref,
    history,
    incident,
    blocks,
    inverse,
    out,
    hown,
    inc,
    mats,
    inv,
    hrecv,
    frecv,
    stack,
    fresh,
    load_sem,
    out_sem,
    send_sem,
    recv_sem,
):
    steps, basis, ports = incident.shape
    depth = history.shape[0]
    nblk = blocks.shape[0]
    chunks = ports // LANES
    items = chunks * steps
    slots = depth + steps - 1
    r = lax.axis_index("px")
    c = lax.axis_index("py")
    has_up, has_down = r > 0, r < rows - 1
    has_left, has_right = c > 0, c < cols - 1
    up, down, left, right = (r - 1, c), (r + 1, c), (r, c - 1), (r, c + 1)

    barrier = pltpu.get_barrier_semaphore()
    for here, peer in ((has_up, up), (has_down, down), (has_left, left), (has_right, right)):

        @pl.when(here)
        def _():
            pl.semaphore_signal(barrier, inc=1, device_id=peer, device_id_type=MESH)

    loads = []
    for k in range(chunks):
        loads.append(
            pltpu.make_async_copy(
                history.at[:, :, pl.ds(k * LANES, LANES)], hown.at[k], load_sem.at[k]
            )
        )
    loads.append(pltpu.make_async_copy(blocks, mats, load_sem.at[chunks]))
    loads.append(pltpu.make_async_copy(inverse, inv, load_sem.at[chunks + 1]))
    for k in range(chunks):
        loads.append(
            pltpu.make_async_copy(
                incident.at[:, :, pl.ds(k * LANES, LANES)], inc.at[k], load_sem.at[chunks + 2 + k]
            )
        )
    for load in loads:
        load.start()

    def copy(src, dst, item, way, slot, peer):
        return pltpu.make_async_remote_copy(
            src_ref=src,
            dst_ref=dst,
            send_sem=send_sem.at[item * 8 + way],
            recv_sem=recv_sem.at[item * 9 + slot],
            device_id=peer,
            device_id_type=MESH,
        )

    def own_ways():
        return (
            (0, has_down, down, 1),
            (1, has_up, up, 7),
            (2, has_right, right, 3),
            (3, has_left, left, 5),
        )

    def relay_ways():
        return (
            (4, has_up, 1, has_right, right, 0),
            (5, has_up, 1, has_left, left, 2),
            (6, has_down, 7, has_right, right, 6),
            (7, has_down, 7, has_left, left, 8),
        )

    def send(src, buffer, part, item):
        for way, here, peer, slot in own_ways():

            @pl.when(here)
            def _():
                copy(src, buffer.at[part, slot], item, way, slot, peer).start()

    def landed(buffer, part, item, slot):
        copy(buffer.at[part, slot], buffer.at[part, slot], item, 0, slot, up).wait_recv()

    def relay(buffer, part, item):
        for here, slot in ((has_up, 1), (has_down, 7)):

            @pl.when(here)
            def _():
                landed(buffer, part, item, slot)
                for way, _a, source, side, peer, target in relay_ways():
                    if source == slot:

                        @pl.when(side)
                        def _():
                            copy(
                                buffer.at[part, source],
                                buffer.at[part, target],
                                item,
                                way,
                                target,
                                peer,
                            ).start()

    def stencil():
        both = jnp.logical_and
        return (
            (0, both(has_up, has_left)),
            (1, has_up),
            (2, both(has_up, has_right)),
            (3, has_left),
            (5, has_right),
            (6, both(has_down, has_left)),
            (7, has_down),
            (8, both(has_down, has_right)),
        )

    for slot, here in stencil():

        @pl.when(jnp.logical_not(here))
        def _():
            def clear(i, carry):
                stack[i * 9 + slot] = jnp.zeros((basis, LANES), stack.dtype)
                return carry

            lax.fori_loop(0, chunks * slots, clear, 0)

    degree = (
        has_up.astype(jnp.int32)
        + has_down.astype(jnp.int32)
        + has_left.astype(jnp.int32)
        + has_right.astype(jnp.int32)
    )
    pl.semaphore_wait(barrier, degree)

    for k in range(chunks):
        loads[k].wait()
        send(hown.at[k], hrecv, k, k)
    for load in loads[chunks:]:
        load.wait()
    for k in range(chunks):
        for d in range(depth):
            stack[(k * slots + d) * 9 + 4] = hown[k, d]
    relay(hrecv, 0, 0)

    def body(q, carry):
        s = q // chunks
        k = q - s * chunks

        @pl.when(q + 1 < chunks)
        def _():
            relay(hrecv, q + 1, q + 1)

        @pl.when(jnp.logical_and(q + 1 >= chunks, q + 1 < items))
        def _():
            relay(frecv, q + 1 - chunks, q + 1)

        @pl.when(q < chunks)
        def _():
            for slot, here in stencil():

                @pl.when(here)
                def _():
                    if slot not in (1, 7):
                        landed(hrecv, q, q, slot)
                    for d in range(depth):
                        stack[(k * slots + d) * 9 + slot] = hrecv[q, slot, d]

        @pl.when(q >= chunks)
        def _():
            for slot, here in stencil():

                @pl.when(here)
                def _():
                    if slot not in (1, 7):
                        landed(frecv, q - chunks, q, slot)
                    stack[(k * slots + depth + s - 1) * 9 + slot] = frecv[q - chunks, slot]

        field = jnp.zeros((basis, LANES), jnp.float32)
        for j in range(0, nblk, GROUP):
            sources = []
            for i in range(j, j + GROUP):
                lag = jnp.maximum(lag_ref[i], 1)
                frame = jnp.where(s < lag, lag - s - 1, depth + s - lag)
                sources.append(stack[(k * slots + frame) * 9 + near_ref[i]])
            field = field + jnp.dot(
                jnp.concatenate([mats[i] for i in range(j, j + GROUP)], axis=1),
                jnp.concatenate(sources, axis=0),
                preferred_element_type=jnp.float32,
            )
        rhs = inc[k, s] - field
        current = jnp.dot(
            inv[...], rhs, precision=lax.Precision.HIGHEST, preferred_element_type=jnp.float32
        ).astype(jnp.bfloat16)
        fresh[q] = current

        @pl.when(s + 1 < steps)
        def _():
            stack[(k * slots + depth + s) * 9 + 4] = current
            send(fresh.at[q], frecv, q, q + chunks)

        pltpu.make_async_copy(
            fresh.at[q],
            out.at[s, :, pl.ds(pl.multiple_of(k * LANES, LANES), LANES)],
            out_sem.at[q],
        ).start()
        return carry

    lax.fori_loop(0, items, body, 0)

    def finish(q, carry):
        s = q // chunks
        k = q - s * chunks
        pltpu.make_async_copy(
            fresh.at[q],
            out.at[s, :, pl.ds(pl.multiple_of(k * LANES, LANES), LANES)],
            out_sem.at[q],
        ).wait()

        def drain(src, dst):
            for way, here, peer, slot in own_ways():

                @pl.when(here)
                def _():
                    copy(src, dst.at[slot], q, way, slot, peer).wait_send()

            for way, here, source, side, peer, target in relay_ways():

                @pl.when(jnp.logical_and(here, side))
                def _():
                    copy(dst.at[source], dst.at[target], q, way, target, peer).wait_send()

        @pl.when(q < chunks)
        def _():
            drain(hown.at[q], hrecv.at[q])

        @pl.when(q >= chunks)
        def _():
            drain(fresh.at[q - chunks], frecv.at[q - chunks])

        return carry

    lax.fori_loop(0, items, finish, 0)


def local(rows, cols, history, incident, blocks, self_inverse, neighbour, delay):
    depth, basis, ports = history.shape[2:]
    steps = incident.shape[2]
    nblk = blocks.shape[2]
    chunks = ports // LANES
    items = chunks * steps
    slots = depth + steps - 1
    later = items - chunks
    smem = pl.BlockSpec(memory_space=pltpu.SMEM)
    hbm = pl.BlockSpec(memory_space=pl.ANY)
    half = jnp.bfloat16
    currents = pl.pallas_call(
        functools.partial(kernel, rows, cols),
        out_shape=jax.ShapeDtypeStruct((steps, basis, ports), half),
        in_specs=[smem, smem, hbm, hbm, hbm, hbm],
        out_specs=hbm,
        scratch_shapes=[
            pltpu.VMEM((chunks, depth, basis, LANES), half),
            pltpu.VMEM((chunks, steps, basis, LANES), jnp.float32),
            pltpu.VMEM((nblk, basis, basis), half),
            pltpu.VMEM((basis, basis), jnp.float32),
            pltpu.VMEM((chunks, 9, depth, basis, LANES), half),
            pltpu.VMEM((later, 9, basis, LANES), half),
            pltpu.VMEM((chunks * slots * 9, basis, LANES), half),
            pltpu.VMEM((items, basis, LANES), half),
            pltpu.SemaphoreType.DMA((2 * chunks + 2,)),
            pltpu.SemaphoreType.DMA((items,)),
            pltpu.SemaphoreType.DMA((items * 8,)),
            pltpu.SemaphoreType.DMA((items * 9,)),
        ],
        compiler_params=pltpu.CompilerParams(
            collective_id=0, has_side_effects=True, vmem_limit_bytes=48 * 1024 * 1024
        ),
    )(
        neighbour[0, 0],
        delay[0, 0],
        history[0, 0],
        incident[0, 0],
        blocks[0, 0],
        self_inverse[0, 0],
    )
    return currents[None, None]


def solution(mesh):
    in_specs = (
        P("px", "py", None, None, None),
        P("px", "py", None, None, None),
        P("px", "py", None, None, None),
        P("px", "py", None, None),
        P("px", "py", None),
        P("px", "py", None),
    )
    out_specs = P("px", "py", None, None, None)
    body = functools.partial(local, mesh.shape["px"], mesh.shape["py"])
    return jax.shard_map(body, mesh=mesh, in_specs=in_specs, out_specs=out_specs, check_vma=False)
```

time: 155 us -> 52.4 us (0.34)
  starting transfers between devices: 50.1 us -> 0 us
  Pallas kernels: 0 us -> 46 us
  waiting for transfers between devices: 41.3 us -> 0 us
  local copies, waits for them, and re-layouts: 29.1 us -> 5.57 us
  other arithmetic: 19.1 us -> 0 us
  matrix products: 12.9 us -> 0 us
    ppermute x16 -> x0, starting transfers between devices: 50.1 us -> none  [the longest x8 31 us: extended(): lax.ppermute(tail, axis, [(i, (i + 1) % count) for i in range(ends)])]
    pallas_call x0 -> x1, Pallas kernels: none -> 46 us  [local(): pl.pallas_call(functools.partial(kernel, rows, cols), out_shape=jax.Shape...]
    ppermute x16 -> x0, waiting for transfers between devices: 41.3 us -> none  [the longest x8 25.8 us: extended(): lax.ppermute(head, axis, [((i + 1) % count, i) for i in range(ends)])]
    gather x4 -> x0, local copies, waits for them, and re-layouts: 19.1 us -> none  [local(): sources = jnp.take(flat, index, axis=0)]
    concatenate x8 -> x0, other arithmetic: 14.5 us -> none  [the longest x3 12.6 us: local(): stack = jnp.concatenate(frames, axis=2)]
    dot_general x8 -> x0, matrix products: 12.9 us -> none  [the longest x4 10.9 us: local(): jnp.einsum('jab,jbp->ap', matrix, sources, preferred_element_type=jnp.flo...]
    broadcast_in_dim x4 -> x0, local copies, waits for them, and re-layouts: 7.94 us -> none  [the longest x3 7.01 us: local(): frames.append(spread_fresh(current[None, None])[:, :, None])]
    unnamed x22 -> x13, local copies, waits for them, and re-layouts: 1.04 us -> 5.57 us
  transfers between devices with their start and end apart: 16 -> 0, of which waited for: 16 -> 0; matrix products, arithmetic and copies ran while one was open for 1% -> 0% of each run, Pallas kernels for 0% -> 0%
where the time goes in v1:
time: 52.4 us; the launch traced here: 51.6 us
  Pallas kernels  46 us (88%)
  local copies, waits for them, and re-layouts  5.57 us (11%)
    pallas_call x1, Pallas kernels, local(): pl.pallas_call(functools.partial(kernel, rows, cols), out_shape=jax.Shape...  46 us
    unnamed x13, local copies, waits for them, and re-layouts  5.57 us

profile of v1, /device:TPU:9, one launch (start us, length us, event | category | flops | bytes accessed | tf_op | source)
XLA Modules:
  0.0 51.6 jit_solution(6646903781654365916)
XLA Ops:
  0.0 0.0 copy-start.4
  0.0 0.0 copy-start.5
  0.0 0.7 %copy-done.4 = s32[1,1,32]{2,1,0:T(1,128)S(1)} copy-done((s32[1,1,32]{2,1,0:T(1,128)S(1)}, s32[1,1,32]{2,1,0:T(1,128)}, u32[]{:S(2)}) %copy-start.4) | copy-done | bytes 152
  0.7 0.0 copy-done.5
  0.7 0.0 copy-start
  0.7 1.2 %copy-done = bf16[1,1,32,128,128]{4,3,2,1,0:T(8,128)(2,1)S(1)} copy-done((bf16[1,1,32,128,128]{4,3,2,1,0:T(8,128)(2,1)S(1)}, bf16[1,1,32,128,128]{4,3,2,1,0:T(8,128)(2,1)}, u32[]{:S(2)}) %copy-start) | copy-done | bytes 1048600
  1.9 0.0 copy-start.1
  1.9 1.1 %copy-done.1 = f32[1,1,4,128,384]{4,3,2,1,0:T(8,128)S(1)} copy-done((f32[1,1,4,128,384]{4,3,2,1,0:T(8,128)S(1)}, f32[1,1,4,128,384]{4,3,2,1,0:T(8,128)}, u32[]{:S(2)}) %copy-start.1) | copy-done | bytes 786456
  3.0 0.0 copy-start.2
  3.0 1.0 %copy-done.2 = bf16[1,1,3,128,384]{4,3,2,1,0:T(8,128)(2,1)S(1)} copy-done((bf16[1,1,3,128,384]{4,3,2,1,0:T(8,128)(2,1)S(1)}, bf16[1,1,3,128,384]{4,3,2,1,0:T(8,128)(2,1)}, u32[]{:S(2)}) %copy-start.2) | copy-done | bytes 294936
  4.0 0.0 copy-start.3
  4.0 0.8 %copy-done.3 = f32[1,1,128,128]{3,2,1,0:T(8,128)S(1)} copy-done((f32[1,1,128,128]{3,2,1,0:T(8,128)S(1)}, f32[1,1,128,128]{3,2,1,0:T(8,128)}, u32[]{:S(2)}) %copy-start.3) | copy-done | bytes 65560
  4.8 46.0 %shard_map.64 = bf16[4,128,384]{2,1,0:T(8,128)(2,1)S(1)} custom-call(s32[32]{0:T(128)S(1)} %bitcast.12, s32[32]{0:T(128)S(1)} %bitcast.13, bf16[3,128,384]{2,1,0:T(8,128)(2,1)S(1)} %bitcast.10, f32[4,128,384]{2,1,0:T(8,128)S(1)} %bitcast.9, bf16[32,128,128]{2,1,0:T(8,128)(2,1)S(1)} %bitcast.8, f32[128,128]{1,0:T(8,128)S(1)} %bitcast.11), custom_call_target="tpu_custom_call" | custom-call | tf_op jit(solution)/shard_map/pallas_call | solution.py:283
  50.9 0.7 %copy.8 = bf16[1,1,4,128,384]{4,3,2,1,0:T(8,128)(2,1)} copy(bf16[1,1,4,128,384]{4,3,2,1,0:T(8,128)(2,1)S(1)} %bitcast.7) | data formatting | bytes 786432
Async XLA Ops:
  0.0 0.7 %copy-start.4 = (s32[1,1,32]{2,1,0:T(1,128)S(1)}, s32[1,1,32]{2,1,0:T(1,128)}, u32[]{:S(2)}) copy-start(s32[1,1,32]{2,1,0:T(1,128)} %param.10) | copy-start | bytes 388
  0.0 0.7 %copy-start.5 = (s32[1,1,32]{2,1,0:T(1,128)S(1)}, s32[1,1,32]{2,1,0:T(1,128)}, u32[]{:S(2)}) copy-start(s32[1,1,32]{2,1,0:T(1,128)} %param.11) | copy-start | bytes 388
  0.7 1.2 %copy-start = (bf16[1,1,32,128,128]{4,3,2,1,0:T(8,128)(2,1)S(1)}, bf16[1,1,32,128,128]{4,3,2,1,0:T(8,128)(2,1)}, u32[]{:S(2)}) copy-start(bf16[1,1,32,128,128]{4,3,2,1,0:T(8,128)(2,1)} %param.8) | copy-start | bytes 3145732
  1.9 1.1 %copy-start.1 = (f32[1,1,4,128,384]{4,3,2,1,0:T(8,128)S(1)}, f32[1,1,4,128,384]{4,3,2,1,0:T(8,128)}, u32[]{:S(2)}) copy-start(f32[1,1,4,128,384]{4,3,2,1,0:T(8,128)} %param.7) | copy-start | bytes 2359300
  3.0 1.0 %copy-start.2 = (bf16[1,1,3,128,384]{4,3,2,1,0:T(8,128)(2,1)S(1)}, bf16[1,1,3,128,384]{4,3,2,1,0:T(8,128)(2,1)}, u32[]{:S(2)}) copy-start(bf16[1,1,3,128,384]{4,3,2,1,0:T(8,128)(2,1)} %param.6) | copy-start | bytes 884740
  4.0 0.8 %copy-start.3 = (f32[1,1,128,128]{3,2,1,0:T(8,128)S(1)}, f32[1,1,128,128]{3,2,1,0:T(8,128)}, u32[]{:S(2)}) copy-start(f32[1,1,128,128]{3,2,1,0:T(8,128)} %param.9) | copy-start | bytes 196612

commit v2 on v1

v2 whole, which is shorter than its diff:
```python
import functools

import jax
import jax.numpy as jnp
from jax import lax
from jax.experimental import pallas as pl
from jax.experimental.pallas import tpu as pltpu
from jax.sharding import PartitionSpec as P

MESH = pl.DeviceIdType.MESH
LANES = 128
GROUP = 4


ROW, ROW_LAG, COLUMN_LAG, WORK = 1.5, 2.5, 3.0, 1.0


def order(chunks, depth, steps):
    now, row_free = 0.0, 0.0
    ready, done, result = [], {}, []

    def launch(k, t):
        nonlocal row_free
        row_free = max(row_free, now) + ROW
        ready.append((row_free + ROW_LAG, "relay", k, t))

    def start(k):
        for t in range(depth):
            result.append(("send", k, t))
            launch(k, t)

    start(0)
    if chunks > 1:
        start(1)
    pending = list(range(2, chunks))
    while ready:
        ready.sort()
        at, kind, k, t = ready.pop(0)
        now = max(now, at)
        result.append((kind, k, t))
        if kind == "relay":
            if t >= depth - 1:
                ready.append((now + COLUMN_LAG, "compute", k, t - depth + 1))
        else:
            now += WORK
            if t + 1 < steps:
                launch(k, depth + t)
            if pending:
                start(pending.pop(0))
    return result


def kernel(
    rows,
    cols,
    near_ref,
    lag_ref,
    history,
    incident,
    blocks,
    inverse,
    out,
    hown,
    inc,
    mats,
    inv,
    split,
    recv,
    stack,
    fresh,
    load_sem,
    out_sem,
    send_sem,
    recv_sem,
):
    steps, basis, ports = incident.shape
    depth = history.shape[0]
    nblk = blocks.shape[0]
    chunks = ports // LANES
    slots = depth + steps - 1
    r = lax.axis_index("px")
    c = lax.axis_index("py")
    has_up, has_down = r > 0, r < rows - 1
    has_left, has_right = c > 0, c < cols - 1
    up, down, left, right = (r - 1, c), (r + 1, c), (r, c - 1), (r, c + 1)

    barrier = pltpu.get_barrier_semaphore()
    for here, peer in ((has_up, up), (has_down, down), (has_left, left), (has_right, right)):

        @pl.when(here)
        def _():
            pl.semaphore_signal(barrier, inc=1, device_id=peer, device_id_type=MESH)

    loads = []
    for k in range(chunks):
        loads.append(
            pltpu.make_async_copy(
                history.at[:, :, pl.ds(k * LANES, LANES)], hown.at[k], load_sem.at[k]
            )
        )
    loads.append(pltpu.make_async_copy(blocks, mats, load_sem.at[chunks]))
    loads.append(pltpu.make_async_copy(inverse, inv, load_sem.at[chunks + 1]))
    for k in range(chunks):
        loads.append(
            pltpu.make_async_copy(
                incident.at[:, :, pl.ds(k * LANES, LANES)], inc.at[k], load_sem.at[chunks + 2 + k]
            )
        )
    for load in loads:
        load.start()

    def copy(src, dst, item, way, slot, peer):
        return pltpu.make_async_remote_copy(
            src_ref=src,
            dst_ref=dst,
            send_sem=send_sem.at[item * 8 + way],
            recv_sem=recv_sem.at[item * 9 + slot],
            device_id=peer,
            device_id_type=MESH,
        )

    own_ways = (
        (0, has_down, down, 1),
        (1, has_up, up, 7),
        (2, has_right, right, 3),
        (3, has_left, left, 5),
    )
    relay_ways = (
        (4, has_up, 1, has_right, right, 0),
        (5, has_up, 1, has_left, left, 2),
        (6, has_down, 7, has_right, right, 6),
        (7, has_down, 7, has_left, left, 8),
    )
    both = jnp.logical_and
    stencil = (
        (0, both(has_up, has_left)),
        (1, has_up),
        (2, both(has_up, has_right)),
        (3, has_left),
        (5, has_right),
        (6, both(has_down, has_left)),
        (7, has_down),
        (8, both(has_down, has_right)),
    )

    def send(src, item):
        for way, here, peer, slot in own_ways:

            @pl.when(here)
            def _():
                copy(src, recv.at[item, slot], item, way, slot, peer).start()

    def landed(item, slot):
        copy(recv.at[item, slot], recv.at[item, slot], item, 0, slot, up).wait_recv()

    def relay(item):
        for here, slot in ((has_up, 1), (has_down, 7)):

            @pl.when(here)
            def _():
                landed(item, slot)
                for way, _a, source, side, peer, target in relay_ways:
                    if source == slot:

                        @pl.when(side)
                        def _():
                            copy(
                                recv.at[item, source],
                                recv.at[item, target],
                                item,
                                way,
                                target,
                                peer,
                            ).start()

    def gather(item):
        for slot, here in stencil:

            @pl.when(here)
            def _():
                if slot not in (1, 7):
                    landed(item, slot)
                stack[item * 9 + slot] = recv[item, slot]

    def output(k, s):
        return pltpu.make_async_copy(
            fresh.at[k, s], out.at[s, :, pl.ds(k * LANES, LANES)], out_sem.at[k * steps + s]
        )

    def compute(k, s):
        if s == 0:
            for t in range(depth):
                gather(k * slots + t)
        else:
            gather(k * slots + depth + s - 1)
        field = jnp.zeros((basis, LANES), jnp.float32)
        for j in range(0, nblk, GROUP):
            sources = []
            for i in range(j, j + GROUP):
                lag = jnp.maximum(lag_ref[i], 1)
                frame = jnp.where(s < lag, lag - s - 1, depth + s - lag)
                sources.append(stack[(k * slots + frame) * 9 + near_ref[i]])
            field = field + jnp.dot(
                jnp.concatenate([mats[i] for i in range(j, j + GROUP)], axis=1),
                jnp.concatenate(sources, axis=0),
                preferred_element_type=jnp.float32,
            )
        rhs = inc[k, s] - field
        high = rhs.astype(jnp.bfloat16)
        low = (rhs - high.astype(jnp.float32)).astype(jnp.bfloat16)
        current = jnp.dot(
            split[...],
            jnp.concatenate([high, low, high], axis=0),
            preferred_element_type=jnp.float32,
        ).astype(jnp.bfloat16)
        fresh[k, s] = current
        if s + 1 < steps:
            item = k * slots + depth + s
            send(fresh.at[k, s], item)
            stack[item * 9 + 4] = current
        output(k, s).start()

    degree = (
        has_up.astype(jnp.int32)
        + has_down.astype(jnp.int32)
        + has_left.astype(jnp.int32)
        + has_right.astype(jnp.int32)
    )
    pl.semaphore_wait(barrier, degree)

    first = True
    for kind, k, t in order(chunks, depth, steps):
        item = k * slots + t
        if kind == "send":
            if t == 0:
                loads[k].wait()
            send(hown.at[k, t], item)
        if kind == "relay":
            if first:
                first = False
                for slot, here in stencil:

                    @pl.when(jnp.logical_not(here))
                    def _():
                        def clear(i, carry):
                            stack[i * 9 + slot] = jnp.zeros((basis, LANES), stack.dtype)
                            return carry

                        lax.fori_loop(0, chunks * slots, clear, 0)

                for load in loads[chunks:]:
                    load.wait()
                whole = inv[...]
                high = whole.astype(jnp.bfloat16)
                low = (whole - high.astype(jnp.float32)).astype(jnp.bfloat16)
                split[...] = jnp.concatenate([high, high, low], axis=1)
            relay(item)
        if kind == "compute":
            if t == 0:
                for d in range(depth):
                    stack[(k * slots + d) * 9 + 4] = hown[k, d]
            compute(k, t)

    for k in range(chunks):
        for s in range(steps):
            output(k, s).wait()

    def finish(item, carry):
        for way, here, peer, slot in own_ways:

            @pl.when(here)
            def _():
                copy(fresh.at[0, 0], recv.at[item, slot], item, way, slot, peer).wait_send()

        for way, here, source, side, peer, target in relay_ways:

            @pl.when(both(here, side))
            def _():
                copy(
                    recv.at[item, source], recv.at[item, target], item, way, target, peer
                ).wait_send()

        return carry

    lax.fori_loop(0, chunks * slots, finish, 0)


def local(rows, cols, history, incident, blocks, self_inverse, neighbour, delay):
    depth, basis, ports = history.shape[2:]
    steps = incident.shape[2]
    nblk = blocks.shape[2]
    chunks = ports // LANES
    items = chunks * steps
    slots = depth + steps - 1
    smem = pl.BlockSpec(memory_space=pltpu.SMEM)
    hbm = pl.BlockSpec(memory_space=pltpu.HBM)
    half = jnp.bfloat16
    currents = pl.pallas_call(
        functools.partial(kernel, rows, cols),
        out_shape=jax.ShapeDtypeStruct((steps, basis, ports), half),
        in_specs=[smem, smem, hbm, hbm, hbm, hbm],
        out_specs=pl.BlockSpec(memory_space=pl.ANY),
        scratch_shapes=[
            pltpu.VMEM((chunks, depth, basis, LANES), half),
            pltpu.VMEM((chunks, steps, basis, LANES), jnp.float32),
            pltpu.VMEM((nblk, basis, basis), half),
            pltpu.VMEM((basis, basis), jnp.float32),
            pltpu.VMEM((basis, 3 * basis), half),
            pltpu.VMEM((chunks * slots, 9, basis, LANES), half),
            pltpu.VMEM((chunks * slots * 9, basis, LANES), half),
            pltpu.VMEM((chunks, steps, basis, LANES), half),
            pltpu.SemaphoreType.DMA((2 * chunks + 2,)),
            pltpu.SemaphoreType.DMA((items,)),
            pltpu.SemaphoreType.DMA((chunks * slots * 8,)),
            pltpu.SemaphoreType.DMA((chunks * slots * 9,)),
        ],
        compiler_params=pltpu.CompilerParams(
            collective_id=0, has_side_effects=True, vmem_limit_bytes=48 * 1024 * 1024
        ),
    )(
        neighbour[0, 0],
        delay[0, 0],
        history[0, 0],
        incident[0, 0],
        blocks[0, 0],
        self_inverse[0, 0],
    )
    return currents[None, None]


def solution(mesh):
    in_specs = (
        P("px", "py", None, None, None),
        P("px", "py", None, None, None),
        P("px", "py", None, None, None),
        P("px", "py", None, None),
        P("px", "py", None),
        P("px", "py", None),
    )
    out_specs = P("px", "py", None, None, None)
    body = functools.partial(local, mesh.shape["px"], mesh.shape["py"])
    return jax.shard_map(body, mesh=mesh, in_specs=in_specs, out_specs=out_specs, check_vma=False)
```

time: 52.4 us -> 59.2 us (1.13)
  Pallas kernels: 46 us -> 52.8 us
    pallas_call x1, Pallas kernels: 46 us -> 52.8 us  [local(): pl.pallas_call(functools.partial(kernel, rows, cols), out_shape=jax.Shape...]
where the time goes in v2:
time: 59.2 us; the launch traced here: 58.4 us
  Pallas kernels  52.8 us (89%)
  local copies, waits for them, and re-layouts  5.57 us (9%)
    pallas_call x1, Pallas kernels, local(): pl.pallas_call(functools.partial(kernel, rows, cols), out_shape=jax.Shape...  52.8 us
    unnamed x13, local copies, waits for them, and re-layouts  5.57 us

profile of v2, /device:TPU:9, one launch (start us, length us, event | category | flops | bytes accessed | tf_op | source)
XLA Modules:
  0.0 58.4 jit_solution(16855949210512952348)
XLA Ops:
  0.0 0.0 copy-start.4
  0.0 0.0 copy-start.5
  0.0 0.7 %copy-done.4 = s32[1,1,32]{2,1,0:T(1,128)S(1)} copy-done((s32[1,1,32]{2,1,0:T(1,128)S(1)}, s32[1,1,32]{2,1,0:T(1,128)}, u32[]{:S(2)}) %copy-start.4) | copy-done | bytes 152
  0.7 0.0 copy-done.5
  0.7 0.0 copy-start
  0.7 1.2 %copy-done = bf16[1,1,32,128,128]{4,3,2,1,0:T(8,128)(2,1)S(1)} copy-done((bf16[1,1,32,128,128]{4,3,2,1,0:T(8,128)(2,1)S(1)}, bf16[1,1,32,128,128]{4,3,2,1,0:T(8,128)(2,1)}, u32[]{:S(2)}) %copy-start) | copy-done | bytes 1048600
  1.9 0.0 copy-start.1
  1.9 1.1 %copy-done.1 = f32[1,1,4,128,384]{4,3,2,1,0:T(8,128)S(1)} copy-done((f32[1,1,4,128,384]{4,3,2,1,0:T(8,128)S(1)}, f32[1,1,4,128,384]{4,3,2,1,0:T(8,128)}, u32[]{:S(2)}) %copy-start.1) | copy-done | bytes 786456
  3.0 0.0 copy-start.2
  3.0 1.0 %copy-done.2 = bf16[1,1,3,128,384]{4,3,2,1,0:T(8,128)(2,1)S(1)} copy-done((bf16[1,1,3,128,384]{4,3,2,1,0:T(8,128)(2,1)S(1)}, bf16[1,1,3,128,384]{4,3,2,1,0:T(8,128)(2,1)}, u32[]{:S(2)}) %copy-start.2) | copy-done | bytes 294936
  4.0 0.0 copy-start.3
  4.0 0.8 %copy-done.3 = f32[1,1,128,128]{3,2,1,0:T(8,128)S(1)} copy-done((f32[1,1,128,128]{3,2,1,0:T(8,128)S(1)}, f32[1,1,128,128]{3,2,1,0:T(8,128)}, u32[]{:S(2)}) %copy-start.3) | copy-done | bytes 65560
  4.8 52.8 %shard_map.64 = bf16[4,128,384]{2,1,0:T(8,128)(2,1)S(1)} custom-call(s32[32]{0:T(128)S(1)} %bitcast.12, s32[32]{0:T(128)S(1)} %bitcast.13, bf16[3,128,384]{2,1,0:T(8,128)(2,1)S(1)} %bitcast.10, f32[4,128,384]{2,1,0:T(8,128)S(1)} %bitcast.9, bf16[32,128,128]{2,1,0:T(8,128)(2,1)S(1)} %bitcast.8, f32[128,128]{1,0:T(8,128)S(1)} %bitcast.11), custom_call_target="tpu_custom_call" | custom-call | tf_op jit(solution)/shard_map/pallas_call | solution.py:298
  57.6 0.7 %copy.8 = bf16[1,1,4,128,384]{4,3,2,1,0:T(8,128)(2,1)} copy(bf16[1,1,4,128,384]{4,3,2,1,0:T(8,128)(2,1)S(1)} %bitcast.7) | data formatting | bytes 786432
Async XLA Ops:
  0.0 0.7 %copy-start.4 = (s32[1,1,32]{2,1,0:T(1,128)S(1)}, s32[1,1,32]{2,1,0:T(1,128)}, u32[]{:S(2)}) copy-start(s32[1,1,32]{2,1,0:T(1,128)} %param.10) | copy-start | bytes 388
  0.0 0.7 %copy-start.5 = (s32[1,1,32]{2,1,0:T(1,128)S(1)}, s32[1,1,32]{2,1,0:T(1,128)}, u32[]{:S(2)}) copy-start(s32[1,1,32]{2,1,0:T(1,128)} %param.11) | copy-start | bytes 388
  0.7 1.2 %copy-start = (bf16[1,1,32,128,128]{4,3,2,1,0:T(8,128)(2,1)S(1)}, bf16[1,1,32,128,128]{4,3,2,1,0:T(8,128)(2,1)}, u32[]{:S(2)}) copy-start(bf16[1,1,32,128,128]{4,3,2,1,0:T(8,128)(2,1)} %param.8) | copy-start | bytes 3145732
  1.9 1.1 %copy-start.1 = (f32[1,1,4,128,384]{4,3,2,1,0:T(8,128)S(1)}, f32[1,1,4,128,384]{4,3,2,1,0:T(8,128)}, u32[]{:S(2)}) copy-start(f32[1,1,4,128,384]{4,3,2,1,0:T(8,128)} %param.7) | copy-start | bytes 2359300
  3.0 1.0 %copy-start.2 = (bf16[1,1,3,128,384]{4,3,2,1,0:T(8,128)(2,1)S(1)}, bf16[1,1,3,128,384]{4,3,2,1,0:T(8,128)(2,1)}, u32[]{:S(2)}) copy-start(bf16[1,1,3,128,384]{4,3,2,1,0:T(8,128)(2,1)} %param.6) | copy-start | bytes 884740
  4.0 0.8 %copy-start.3 = (f32[1,1,128,128]{3,2,1,0:T(8,128)S(1)}, f32[1,1,128,128]{3,2,1,0:T(8,128)}, u32[]{:S(2)}) copy-start(f32[1,1,128,128]{3,2,1,0:T(8,128)} %param.9) | copy-start | bytes 196612

commit v3 on v1

--- a/solution.py
+++ b/solution.py
@@ -26,6 +26,7 @@
     inc,
     mats,
     inv,
+    split,
     hrecv,
     frecv,
     stack,
@@ -84,10 +85,10 @@
 
     def own_ways():
         return (
+            (2, has_right, right, 3),
+            (3, has_left, left, 5),
             (0, has_down, down, 1),
             (1, has_up, up, 7),
-            (2, has_right, right, 3),
-            (3, has_left, left, 5),
         )
 
     def relay_ways():
@@ -164,22 +165,24 @@
         send(hown.at[k], hrecv, k, k)
     for load in loads[chunks:]:
         load.wait()
+    whole = inv[...]
+    high = whole.astype(jnp.bfloat16)
+    low = (whole - high.astype(jnp.float32)).astype(jnp.bfloat16)
+    split[...] = jnp.concatenate([high, high, low], axis=1)
     for k in range(chunks):
         for d in range(depth):
             stack[(k * slots + d) * 9 + 4] = hown[k, d]
-    relay(hrecv, 0, 0)
+    for k in range(chunks):
+        relay(hrecv, k, k)
 
     def body(q, carry):
         s = q // chunks
         k = q - s * chunks
 
-        @pl.when(q + 1 < chunks)
-        def _():
-            relay(hrecv, q + 1, q + 1)
-
-        @pl.when(jnp.logical_and(q + 1 >= chunks, q + 1 < items))
-        def _():
-            relay(frecv, q + 1 - chunks, q + 1)
+        @pl.when(jnp.logical_and(q >= chunks, k == 0))
+        def _():
+            for later in range(chunks):
+                relay(frecv, q - chunks + later, q + later)
 
         @pl.when(q < chunks)
         def _():
@@ -215,8 +218,12 @@
                 preferred_element_type=jnp.float32,
             )
         rhs = inc[k, s] - field
+        high = rhs.astype(jnp.bfloat16)
+        low = (rhs - high.astype(jnp.float32)).astype(jnp.bfloat16)
         current = jnp.dot(
-            inv[...], rhs, precision=lax.Precision.HIGHEST, preferred_element_type=jnp.float32
+            split[...],
+            jnp.concatenate([high, low, high], axis=0),
+            preferred_element_type=jnp.float32,
         ).astype(jnp.bfloat16)
         fresh[q] = current
 
@@ -278,18 +285,19 @@
     slots = depth + steps - 1
     later = items - chunks
     smem = pl.BlockSpec(memory_space=pltpu.SMEM)
-    hbm = pl.BlockSpec(memory_space=pl.ANY)
+    hbm = pl.BlockSpec(memory_space=pltpu.HBM)
     half = jnp.bfloat16
     currents = pl.pallas_call(
         functools.partial(kernel, rows, cols),
         out_shape=jax.ShapeDtypeStruct((steps, basis, ports), half),
         in_specs=[smem, smem, hbm, hbm, hbm, hbm],
-        out_specs=hbm,
+        out_specs=pl.BlockSpec(memory_space=pl.ANY),
         scratch_shapes=[
             pltpu.VMEM((chunks, depth, basis, LANES), half),
             pltpu.VMEM((chunks, steps, basis, LANES), jnp.float32),
             pltpu.VMEM((nblk, basis, basis), half),
             pltpu.VMEM((basis, basis), jnp.float32),
+            pltpu.VMEM((basis, 3 * basis), half),
             pltpu.VMEM((chunks, 9, depth, basis, LANES), half),
             pltpu.VMEM((later, 9, basis, LANES), half),
             pltpu.VMEM((chunks * slots * 9, basis, LANES), half),

time: 52.4 us -> 50.5 us (0.964)
  Pallas kernels: 46 us -> 44.6 us
    pallas_call x1, Pallas kernels: 46 us -> 44.6 us  [local(): pl.pallas_call(functools.partial(kernel, rows, cols), out_shape=jax.Shape...]
where the time goes in v3:
time: 50.5 us; the launch traced here: 50.2 us
  Pallas kernels  44.6 us (88%)
  local copies, waits for them, and re-layouts  5.57 us (11%)
    pallas_call x1, Pallas kernels, local(): pl.pallas_call(functools.partial(kernel, rows, cols), out_shape=jax.Shape...  44.6 us
    unnamed x13, local copies, waits for them, and re-layouts  5.57 us

profile of v3, /device:TPU:9, one launch (start us, length us, event | category | flops | bytes accessed | tf_op | source)
XLA Modules:
  0.0 50.2 jit_solution(2342374625677880644)
XLA Ops:
  0.0 0.0 copy-start.4
  0.0 0.0 copy-start.5
  0.0 0.7 %copy-done.4 = s32[1,1,32]{2,1,0:T(1,128)S(1)} copy-done((s32[1,1,32]{2,1,0:T(1,128)S(1)}, s32[1,1,32]{2,1,0:T(1,128)}, u32[]{:S(2)}) %copy-start.4) | copy-done | bytes 152
  0.7 0.0 copy-done.5
  0.7 0.0 copy-start
  0.7 1.2 %copy-done = bf16[1,1,32,128,128]{4,3,2,1,0:T(8,128)(2,1)S(1)} copy-done((bf16[1,1,32,128,128]{4,3,2,1,0:T(8,128)(2,1)S(1)}, bf16[1,1,32,128,128]{4,3,2,1,0:T(8,128)(2,1)}, u32[]{:S(2)}) %copy-start) | copy-done | bytes 1048600
  1.9 0.0 copy-start.1
  1.9 1.1 %copy-done.1 = f32[1,1,4,128,384]{4,3,2,1,0:T(8,128)S(1)} copy-done((f32[1,1,4,128,384]{4,3,2,1,0:T(8,128)S(1)}, f32[1,1,4,128,384]{4,3,2,1,0:T(8,128)}, u32[]{:S(2)}) %copy-start.1) | copy-done | bytes 786456
  3.0 0.0 copy-start.2
  3.0 1.0 %copy-done.2 = bf16[1,1,3,128,384]{4,3,2,1,0:T(8,128)(2,1)S(1)} copy-done((bf16[1,1,3,128,384]{4,3,2,1,0:T(8,128)(2,1)S(1)}, bf16[1,1,3,128,384]{4,3,2,1,0:T(8,128)(2,1)}, u32[]{:S(2)}) %copy-start.2) | copy-done | bytes 294936
  4.0 0.0 copy-start.3
  4.0 0.8 %copy-done.3 = f32[1,1,128,128]{3,2,1,0:T(8,128)S(1)} copy-done((f32[1,1,128,128]{3,2,1,0:T(8,128)S(1)}, f32[1,1,128,128]{3,2,1,0:T(8,128)}, u32[]{:S(2)}) %copy-start.3) | copy-done | bytes 65560
  4.8 44.6 %shard_map.64 = bf16[4,128,384]{2,1,0:T(8,128)(2,1)S(1)} custom-call(s32[32]{0:T(128)S(1)} %bitcast.12, s32[32]{0:T(128)S(1)} %bitcast.13, bf16[3,128,384]{2,1,0:T(8,128)(2,1)S(1)} %bitcast.10, f32[4,128,384]{2,1,0:T(8,128)S(1)} %bitcast.9, bf16[32,128,128]{2,1,0:T(8,128)(2,1)S(1)} %bitcast.8, f32[128,128]{1,0:T(8,128)S(1)} %bitcast.11), custom_call_target="tpu_custom_call" | custom-call | tf_op jit(solution)/shard_map/pallas_call | solution.py:290
  49.4 0.7 %copy.8 = bf16[1,1,4,128,384]{4,3,2,1,0:T(8,128)(2,1)} copy(bf16[1,1,4,128,384]{4,3,2,1,0:T(8,128)(2,1)S(1)} %bitcast.7) | data formatting | bytes 786432
Async XLA Ops:
  0.0 0.7 %copy-start.4 = (s32[1,1,32]{2,1,0:T(1,128)S(1)}, s32[1,1,32]{2,1,0:T(1,128)}, u32[]{:S(2)}) copy-start(s32[1,1,32]{2,1,0:T(1,128)} %param.10) | copy-start | bytes 388
  0.0 0.7 %copy-start.5 = (s32[1,1,32]{2,1,0:T(1,128)S(1)}, s32[1,1,32]{2,1,0:T(1,128)}, u32[]{:S(2)}) copy-start(s32[1,1,32]{2,1,0:T(1,128)} %param.11) | copy-start | bytes 388
  0.7 1.2 %copy-start = (bf16[1,1,32,128,128]{4,3,2,1,0:T(8,128)(2,1)S(1)}, bf16[1,1,32,128,128]{4,3,2,1,0:T(8,128)(2,1)}, u32[]{:S(2)}) copy-start(bf16[1,1,32,128,128]{4,3,2,1,0:T(8,128)(2,1)} %param.8) | copy-start | bytes 3145732
  1.9 1.1 %copy-start.1 = (f32[1,1,4,128,384]{4,3,2,1,0:T(8,128)S(1)}, f32[1,1,4,128,384]{4,3,2,1,0:T(8,128)}, u32[]{:S(2)}) copy-start(f32[1,1,4,128,384]{4,3,2,1,0:T(8,128)} %param.7) | copy-start | bytes 2359300
  3.0 1.0 %copy-start.2 = (bf16[1,1,3,128,384]{4,3,2,1,0:T(8,128)(2,1)S(1)}, bf16[1,1,3,128,384]{4,3,2,1,0:T(8,128)(2,1)}, u32[]{:S(2)}) copy-start(bf16[1,1,3,128,384]{4,3,2,1,0:T(8,128)(2,1)} %param.6) | copy-start | bytes 884740
  4.0 0.8 %copy-start.3 = (f32[1,1,128,128]{3,2,1,0:T(8,128)S(1)}, f32[1,1,128,128]{3,2,1,0:T(8,128)}, u32[]{:S(2)}) copy-start(f32[1,1,128,128]{3,2,1,0:T(8,128)} %param.9) | copy-start | bytes 196612
